TPU v7x, 128 devices: a whole 4x4x4 slice. The times are simulated.
128 devices in a mesh: req: 16 (over y, x), exp: 8 (over z, core).
Axes of the slice: x: 4, y: 4, z: 4, core: 2. Of those that a mesh axis runs over, the one named last changes fastest.
Arguments:
- attention_out: bfloat16 [2048, 4096], P('req'), may hold values from -6 to 6
- residual: bfloat16 [2048, 4096], P('req', 'exp'), may hold values from -6 to 6
- w_out: bfloat16 [4096, 4096], P('req', 'exp'), may hold values from -0.09375 to 0.09375
- router_w: float32 [4096, 8], P('exp'), may hold values from -0.09375 to 0.09375
- norm_gain: float32 [4096], P('exp'), may hold values from 0.5 to 1.5
- page_pool: bfloat16 [4096, 8, 2048], P('req', None, 'exp'), may hold values from -6 to 6
- page_table: int32 [2048, 2], P('req'), may hold values from 0 to 255, as said below
- cache_len: int32 [2048], P('req'), may hold values from 1 to 16
- came_from: int32 [2048], replicated, may hold values from 0 to 2047, as said below
- routes: int32 [2048, 2], P('req'), may hold values from 0 to 7, all different within a row; in each aligned block of 128 rows (0 to 127, 128 to 255, ...) at most 64 rows name the same one
- w_gate: bfloat16 [16, 4096, 7168], P('req', None, 'exp'), as said below
- w_up: bfloat16 [16, 4096, 7168], P('req', None, 'exp'), as said below
- w_down: bfloat16 [16, 7168, 4096], P('req', 'exp'), as said below
Outputs:
- mixed: float32 [2048, 4096], P('req', 'exp')
- new_pages: bfloat16 [2048, 2, 8, 2048], P('req', None, None, 'exp')
Inputs may be any that keep to these rules, and one draw needn't show every extreme that they name: page_table's entries for the requests of one req group are distinct. came_from is a permutation; from each req group 4 rows go to each of the other 15 groups, each group receives 4 rows from each of them, and all other rows keep their place. `routes`: within the rows of one req group every expert is named by at most 64 rows, and some expert by exactly 64 rows in some group. `w_gate`: slices e and e + 8 along the first dimension are equal. `w_up`: slices e and e + 8 along the first dimension are equal. `w_down`: slices e and e + 8 along the first dimension are equal.
All inputs are finite; a program needn't handle non-finite values.
Results may differ from a plain program's by a relative error of at most 0.0055.
Values may be sent and summed in bfloat16 or wider, within the bound.
A program may use at most 128 MiB of HBM per device.

v0:
```python
import jax
import jax.numpy as jnp
from jax import lax
from jax.sharding import PartitionSpec as P

D = 4096
CAP = 32
MIG_PAIR = 4
EPSILON = 1e-05


def pick_rows(source, row_index, live_slot):
    taken_rows = jnp.take(source, row_index, axis=0)
    return jnp.where(live_slot[:, None], taken_rows, jnp.zeros((), source.dtype))


def body(
    attention_out,
    residual,
    w_out,
    router_w,
    norm_gain,
    page_pool,
    page_table,
    cache_len,
    came_from,
    routes,
    w_gate,
    w_up,
    w_down,
):
    groups = lax.axis_size("req")
    own_group = lax.axis_index("req")
    row_req = attention_out.shape[0]
    rows_all = came_from.shape[0]
    pages_req = page_table.shape[1]
    page_len = page_pool.shape[1]
    kv_slice = page_pool.shape[2]
    experts = groups // 2
    targets = jnp.arange(groups, dtype=jnp.int32)
    local_ids = jnp.arange(row_req, dtype=jnp.int32)
    dest_of = (
        jnp.zeros((rows_all,), jnp.int32).at[came_from].set(jnp.arange(rows_all, dtype=jnp.int32))
    )
    dest_group = dest_of // row_req
    dest_hot = (
        (dest_group[:, None] == targets[None, :]).astype(jnp.int32).reshape(groups, row_req, groups)
    )
    pair_rank = jnp.sum((jnp.cumsum(dest_hot, axis=1) - dest_hot) * dest_hot, axis=2).reshape(
        rows_all
    )
    own_dest = lax.dynamic_slice_in_dim(dest_group, own_group * row_req, row_req)
    own_rank = lax.dynamic_slice_in_dim(pair_rank, own_group * row_req, row_req)
    chosen_send = (
        (own_dest[None, None, :] == targets[:, None, None])
        & (own_rank[None, None, :] == jnp.arange(MIG_PAIR, dtype=jnp.int32)[None, :, None])
        & (targets[:, None, None] != own_group)
    )
    send_index = jnp.sum(jnp.where(chosen_send, local_ids[None, None, :], 0), axis=2).reshape(-1)
    send_live = jnp.any(chosen_send, axis=2).reshape(-1)
    moved_attn, moved_resid = (
        lax.all_to_all(
            pick_rows(attention_out, send_index, send_live),
            "req",
            split_axis=0,
            concat_axis=0,
            tiled=True,
        ),
        lax.all_to_all(
            pick_rows(residual, send_index, send_live),
            "req",
            split_axis=0,
            concat_axis=0,
            tiled=True,
        ),
    )
    new_source = lax.dynamic_slice_in_dim(came_from, own_group * row_req, row_req)
    source_group = new_source // row_req
    stays_home = source_group == own_group
    arrival = jnp.where(
        stays_home,
        new_source - own_group * row_req,
        row_req + source_group * MIG_PAIR + jnp.take(pair_rank, new_source),
    )
    attn_new = jnp.take(jnp.concatenate([attention_out, moved_attn], axis=0), arrival, axis=0)
    resid_new = jnp.take(jnp.concatenate([residual, moved_resid], axis=0), arrival, axis=0)
    projected = jnp.dot(
        attn_new,
        lax.all_gather(w_out, "req", axis=0, tiled=True),
        preferred_element_type=jnp.float32,
    )
    hidden = resid_new.astype(jnp.float32) + projected
    squares = jnp.sum(hidden * hidden, axis=1)
    scaled = hidden * norm_gain[None, :]
    raw_logits = jnp.dot(scaled, router_w, precision=lax.Precision.HIGHEST)
    row_stats = lax.psum(jnp.concatenate([squares[:, None], raw_logits], axis=1), "exp")
    total_sq = row_stats[:, 0]
    inverse = lax.rsqrt(total_sq / D + EPSILON)
    normed = scaled * inverse[:, None]
    logits = row_stats[:, 1:] * inverse[:, None]
    normed_rows = normed.astype(jnp.bfloat16)
    expert_ids = jnp.arange(experts, dtype=jnp.int32)
    chosen = jnp.sum(
        jnp.where(routes[:, :, None] == expert_ids[None, None, :], logits[:, None, :], 0.0), axis=2
    )
    gate_first = jax.nn.sigmoid(chosen[:, 0] - chosen[:, 1])
    gate_second = jax.nn.sigmoid(chosen[:, 1] - chosen[:, 0])
    flat_routes = routes.reshape(-1)
    expert_hot = (flat_routes[:, None] == expert_ids[None, :]).astype(jnp.int32)
    expert_rank = jnp.sum((jnp.cumsum(expert_hot, axis=0) - expert_hot) * expert_hot, axis=1)
    target_dev = flat_routes + experts * (expert_rank % 2)
    slot_index = expert_rank // 2
    assign_ids = jnp.arange(flat_routes.shape[0], dtype=jnp.int32)
    chosen_slot = (target_dev[None, None, :] == targets[:, None, None]) & (
        slot_index[None, None, :] == jnp.arange(CAP, dtype=jnp.int32)[None, :, None]
    )
    slot_source = jnp.sum(
        jnp.where(chosen_slot, assign_ids[None, None, :] // 2, 0), axis=2
    ).reshape(-1)
    slot_live = jnp.any(chosen_slot, axis=2).reshape(-1)
    outgoing = pick_rows(normed_rows, slot_source, slot_live)
    arrived = lax.all_to_all(outgoing, "req", split_axis=0, concat_axis=0, tiled=True)
    rows_full = lax.all_gather(arrived, "exp", axis=1, tiled=True)
    gate_h = jnp.dot(rows_full, w_gate[0], preferred_element_type=jnp.float32)
    up_h = jnp.dot(rows_full, w_up[0], preferred_element_type=jnp.float32)
    active = (jax.nn.silu(gate_h) * up_h).astype(jnp.bfloat16)
    partial_value = lax.optimization_barrier(
        jnp.dot(active, w_down[0], preferred_element_type=jnp.float32).astype(jnp.bfloat16)
    )
    partial_value, page_pool = lax.optimization_barrier((partial_value, page_pool))
    summed_value = lax.psum_scatter(partial_value, "exp", scatter_dimension=1, tiled=True)
    page_rows = jnp.take(page_pool, page_table.reshape(-1), axis=0).reshape(
        row_req, pages_req, page_len, kv_slice
    )
    position = (
        jnp.arange(pages_req, dtype=jnp.int32)[:, None] * page_len
        + jnp.arange(page_len, dtype=jnp.int32)[None, :]
    )
    kept_mask = position[None, :, :] < cache_len[:, None, None]
    page_rows = jnp.where(kept_mask[..., None], page_rows, jnp.zeros((), page_rows.dtype)).reshape(
        row_req, -1
    )
    moved_pages = lax.all_to_all(
        pick_rows(page_rows, send_index, send_live), "req", split_axis=0, concat_axis=0, tiled=True
    )
    new_pages = jnp.take(
        jnp.concatenate([page_rows, moved_pages], axis=0), arrival, axis=0
    ).reshape(row_req, pages_req, page_len, kv_slice)
    lookup = target_dev * CAP + slot_index
    returned = lax.all_to_all(summed_value, "req", split_axis=0, concat_axis=0, tiled=True)
    taken_rows = jnp.take(returned, lookup, axis=0).reshape(row_req, 2, -1).astype(jnp.float32)
    expert_part = gate_first[:, None] * taken_rows[:, 0] + gate_second[:, None] * taken_rows[:, 1]
    mixed = hidden + expert_part
    return (mixed, new_pages)


def solution(mesh):
    in_specs = (
        P("req", None),
        P("req", "exp"),
        P("req", "exp"),
        P("exp", None),
        P("exp"),
        P("req", None, "exp"),
        P("req", None),
        P("req"),
        P(),
        P("req", None),
        P("req", None, "exp"),
        P("req", None, "exp"),
        P("req", "exp", None),
    )
    out_specs = (P("req", "exp"), P("req", None, None, "exp"))
    return jax.shard_map(body, mesh=mesh, in_specs=in_specs, out_specs=out_specs, check_vma=False)
```

profile of v0, /device:TPU:0, one launch (start us, length us, event | category | flops | bytes accessed | tf_op | source)
XLA Modules:
  0.0 224.9 jit_solution(11997066119131765174)
XLA Ops:
  8.6 8.0 %scatter_custom_fusion = s32[2048]{0:T(1024)S(1)} fusion(s32[2048]{0:T(1024)S(1)} %compare_select_fusion.1, s32[2048]{0:T(1024)S(1)} %iota.72, s32[]{:T(128)} %constant.182.clone.1), kind=kCustom, calls=%fused_computation.93 | custom fusion | bytes 8196 | tf_op jit(solution)/shard_map/scatter | solution.py:43
  16.8 2.8 %select_reduce_fusion = s32[16,128]{0,1:T(8,128)S(1)} fusion(s32[16,128]{0,1:T(8,128)S(1)} %copy.115), kind=kOutput, calls=%fused_computation.27 | output fusion | flops 4388864 | bytes 16384 | tf_op jit(solution)/shard_map/jit(cumsum)/reduce_window_sum | solution.py:49
  20.6 1.6 gather_fusion.1
  23.1 7.1 %all-to-all-start = ((bf16[16,4,512]{2,1,0:T(4,128)(2,1)}), bf16[16,4,512]{2,1,0:T(4,128)(2,1)S(1)}, u32[]{:S(2)}, u32[]{:S(2)}) async-start(bf16[16,4,512]{2,1,0:T(4,128)(2,1)} %select_select_fusion.4), calls=%async_computation | async-start | bytes 131072 | tf_op jit(solution)/shard_map/all_to_all | solution.py:69
  38.0 7.0 %all-to-all-start.1 = ((bf16[16,4,4096]{2,1,0:T(4,128)(2,1)}), bf16[16,4,4096]{2,1,0:T(4,128)(2,1)S(1)}, u32[]{:S(2)}, u32[]{:S(2)}) async-start(bf16[16,4,4096]{2,1,0:T(4,128)(2,1)} %all_to_all.38), calls=%async_computation.1 | async-start | bytes 1048576 | tf_op jit(solution)/shard_map/all_to_all | solution.py:62
  46.3 16.4 %all-to-all-done.1 = bf16[16,4,4096]{2,1,0:T(4,128)(2,1)S(1)} async-done(((bf16[16,4,4096]{2,1,0:T(4,128)(2,1)}), bf16[16,4,4096]{2,1,0:T(4,128)(2,1)S(1)}, u32[]{:S(2)}, u32[]{:S(2)}) %all-to-all-start.1) | async-done | bytes 524320 | tf_op jit(solution)/shard_map/all_to_all | solution.py:62
  62.9 1.4 pad_maximum_fusion
  64.2 2.2 gather_fusion.7
  66.4 3.4 %all-gather.3.cloned.1.call-done = bf16[4096,512]{1,0:T(8,128)(2,1)} async-done(((bf16[256,512]{1,0:T(8,128)(2,1)}), bf16[4096,512]{1,0:T(8,128)(2,1)}) %all-gather.3.cloned.1.call-update) | async-done | bytes 4194320 | tf_op jit(solution)/shard_map/all_gather | solution.py:89
  69.8 3.4 %multiply_reduce_fusion = (f32[128]{0:T(128)S(1)}, f32[128,512]{1,0:T(8,128)S(1)}) fusion(bf16[4096,512]{1,0:T(8,128)(2,1)} %all-gather.3.cloned.1.call-done, bf16[128,4096]{1,0:T(8,128)(2,1)} %gather_fusion.7, pred[128]{0:T(512)(128)(4,1)S(1)} %get-tuple-element.8, bf16[128,512]{1,0:T(8,128)(2,1)S(1)} %gather_fusion.2), kind=kOutput, calls=%fused_computation.48 | convolution fusion | flops 537722752 | bytes 5636736 | tf_op jit(solution)/shard_map/dot_general | solution.py:87
  73.5 15.1 %psum.7 = f32[128,9]{0,1:T(8,128)S(1)} all-reduce(f32[128,9]{0,1:T(8,128)S(1)} %pad_maximum_fusion.3), channel_id=1, replica_groups=mesh['req'=16,'exp'=8] {'exp'}, use_global_device_ids=true, to_apply=%region_6.9 | all-reduce | flops 1152 | bytes 9216 | tf_op jit(solution)/shard_map/psum | solution.py:96
  88.7 2.0 gather_fusion.3
  90.9 15.3 %all_to_all.54 = bf16[16,32,512]{2,1,0:T(8,128)(2,1)} all-to-all(bf16[16,32,512]{2,1,0:T(8,128)(2,1)S(1)} %select_select_fusion.3), channel_id=1, replica_groups=mesh['req'=16,'exp'=8] {'req'}, dimensions={0} | all-to-all | bytes 1048576 | tf_op jit(solution)/shard_map/all_to_all | solution.py:122
  106.4 28.4 %all-gather.5.cloned.1.call-done = bf16[512,4096]{1,0:T(8,128)(2,1)} async-done(((bf16[512,512]{1,0:T(8,128)(2,1)}), bf16[512,4096]{1,0:T(8,128)(2,1)}) %all-gather.5.cloned.1.call-update) | async-done | bytes 4194320 | tf_op jit(solution)/shard_map/all_gather | solution.py:123
  134.9 9.8 %fusion.4 = f32[512,896]{1,0:T(8,128)S(1)} fusion(bf16[512,4096]{1,0:T(8,128)(2,1)} %all-gather.5.cloned.1.call-done, bf16[1,4096,896]{2,1,0:T(8,128)(2,1)} %param.27), kind=kOutput, calls=%fused_computation.15 | convolution fusion | flops 3758096384 | bytes 13369344 | tf_op jit(solution)/shard_map/dot_general | solution.py:124
  144.7 16.2 %fusion.6 = bf16[512,4096]{1,0:T(8,128)(2,1)} fusion(bf16[1,896,4096]{2,1,0:T(8,128)(2,1)} %param.29, f32[512,896]{1,0:T(8,128)S(1)} %fusion.4, bf16[512,4096]{1,0:T(8,128)(2,1)} %all-gather.5.cloned.1.call-done, bf16[1,4096,896]{2,1,0:T(8,128)(2,1)} %param.28), kind=kOutput, calls=%fused_computation.17 | convolution fusion | flops 7521042432 | bytes 24903680 | tf_op jit(solution)/shard_map/dot_general | solution.py:128
  166.9 1.4 select_select_fusion
  170.3 6.8 %all-to-all-start.4 = ((bf16[16,4,4096]{2,1,0:T(4,128)(2,1)}), bf16[16,4,4096]{2,1,0:T(4,128)(2,1)S(1)}, u32[]{:S(2)}, u32[]{:S(2)}) async-start(bf16[16,4,4096]{2,1,0:T(4,128)(2,1)} %all_to_all.46), calls=%async_computation.5 | async-start | bytes 1048576 | tf_op jit(solution)/shard_map/all_to_all | solution.py:143
  177.2 11.9 %all-to-all-done.4 = bf16[16,4,4096]{2,1,0:T(4,128)(2,1)S(1)} async-done(((bf16[16,4,4096]{2,1,0:T(4,128)(2,1)}), bf16[16,4,4096]{2,1,0:T(4,128)(2,1)S(1)}, u32[]{:S(2)}, u32[]{:S(2)}) %all-to-all-start.4) | async-done | bytes 524320 | tf_op jit(solution)/shard_map/all_to_all | solution.py:143
  190.6 2.2 gather_fusion.9
  192.8 6.6 %reduce-scatter.2.cloned.1.call-done = bf16[512,512]{1,0:T(8,128)(2,1)} async-done(((bf16[512,4096]{1,0:T(8,128)(2,1)}), bf16[512,512]{1,0:T(8,128)(2,1)}) %reduce-scatter.2.cloned.1.call-update) | async-done | bytes 524304 | tf_op jit(solution)/shard_map/reduce_scatter | solution.py:131
  199.3 6.7 %all-to-all-start.3 = ((bf16[16,32,512]{2,1,0:T(8,128)(2,1)}), bf16[16,32,512]{2,1,0:T(8,128)(2,1)S(1)}, u32[]{:S(2)}, u32[]{:S(2)}) async-start(bf16[16,32,512]{2,1,0:T(8,128)(2,1)} %bitcast.81), calls=%async_computation.4 | async-start | bytes 1048576 | tf_op jit(solution)/shard_map/all_to_all | solution.py:150
  206.0 1.4 broadcast_select_fusion
  208.6 7.5 %all-to-all-done.3 = bf16[16,32,512]{2,1,0:T(8,128)(2,1)S(1)} async-done(((bf16[16,32,512]{2,1,0:T(8,128)(2,1)}), bf16[16,32,512]{2,1,0:T(8,128)(2,1)S(1)}, u32[]{:S(2)}, u32[]{:S(2)}) %all-to-all-start.3) | async-done | bytes 524320 | tf_op jit(solution)/shard_map/all_to_all | solution.py:150
  (121 shorter events, 26.1 us)
Async XLA Ops:
  7.2 158.4 %copy-start = (bf16[256,8,256]{2,1,0:T(8,128)(2,1)S(1)}, bf16[256,8,256]{2,1,0:T(8,128)(2,1)}, u32[]{:S(2)}) copy-start(bf16[256,8,256]{2,1,0:T(8,128)(2,1)} %param.22) | copy-start | bytes 3145732
  7.2 24.4 %copy-start.2 = (bf16[128,4096]{1,0:T(8,128)(2,1)S(1)}, bf16[128,4096]{1,0:T(8,128)(2,1)}, u32[]{:S(2)}) copy-start(bf16[128,4096]{1,0:T(8,128)(2,1)} %param.17) | copy-start | bytes 3145732
  7.2 62.6 %all-gather.3.cloned.1.call-start = ((), (), s32[]{:S(2)}) async-start(), calls=%async_computation.6 | async-start | bytes 4456448 | tf_op jit(solution)/shard_map/all_gather | solution.py:89
  23.1 14.9 %all-to-all-start = ((bf16[16,4,512]{2,1,0:T(4,128)(2,1)}), bf16[16,4,512]{2,1,0:T(4,128)(2,1)S(1)}, u32[]{:S(2)}, u32[]{:S(2)}) async-start(bf16[16,4,512]{2,1,0:T(4,128)(2,1)} %select_select_fusion.4), calls=%async_computation | async-start | bytes 131072 | tf_op jit(solution)/shard_map/all_to_all | solution.py:69
  31.5 13.9 %copy-start.3 = (bf16[128,512]{1,0:T(8,128)(2,1)S(1)}, bf16[128,512]{1,0:T(8,128)(2,1)}, u32[]{:S(2)}) copy-start(bf16[128,512]{1,0:T(8,128)(2,1)} %param.18) | copy-start | bytes 393220
  38.0 24.7 %all-to-all-start.1 = ((bf16[16,4,4096]{2,1,0:T(4,128)(2,1)}), bf16[16,4,4096]{2,1,0:T(4,128)(2,1)S(1)}, u32[]{:S(2)}, u32[]{:S(2)}) async-start(bf16[16,4,4096]{2,1,0:T(4,128)(2,1)} %all_to_all.38), calls=%async_computation.1 | async-start | bytes 1048576 | tf_op jit(solution)/shard_map/all_to_all | solution.py:62
  45.0 89.9 %all-gather.5.cloned.1.call-start = ((), (), s32[]{:S(2)}) async-start(), calls=%async_computation.7 | async-start | bytes 4718592 | tf_op jit(solution)/shard_map/all_gather | solution.py:123
  66.4 6.8 %copy-start.4 = (f32[512,8]{0,1:T(8,128)S(1)}, f32[512,8]{0,1:T(8,128)}, u32[]{:S(2)}) copy-start(f32[512,8]{0,1:T(8,128)} %param.20) | copy-start | bytes 49156
  66.4 6.8 %copy-start.6 = (f32[512]{0:T(512)S(1)}, f32[512]{0:T(512)}, u32[]{:S(2)}) copy-start(f32[512]{0:T(512)} %param.21) | copy-start | bytes 6148
  106.2 93.1 %reduce-scatter.2.cloned.1.call-start = ((), (), s32[]{:S(2)}) async-start(), calls=%async_computation.8 | async-start | bytes 4718592 | tf_op jit(solution)/shard_map/reduce_scatter | solution.py:131
  160.9 0.7 copy-start.7
  160.9 1.0 copy-start.8
  160.9 4.6 %copy-start.5 = (s32[128,2]{0,1:T(2,128)S(1)}, s32[128,2]{0,1:T(2,128)}, u32[]{:S(2)}) copy-start(s32[128,2]{0,1:T(2,128)} %param.26) | copy-start | bytes 3076
  168.3 20.8 %copy-start.1 = (bf16[128,4096]{1,0:T(8,128)(2,1)}, bf16[128,4096]{1,0:T(8,128)(2,1)S(1)}, u32[]{:S(2)}) copy-start(bf16[128,4096]{1,0:T(8,128)(2,1)S(1)} %select_select_fusion) | copy-start | bytes 3145732
  170.3 18.8 %all-to-all-start.4 = ((bf16[16,4,4096]{2,1,0:T(4,128)(2,1)}), bf16[16,4,4096]{2,1,0:T(4,128)(2,1)S(1)}, u32[]{:S(2)}, u32[]{:S(2)}) async-start(bf16[16,4,4096]{2,1,0:T(4,128)(2,1)} %all_to_all.46), calls=%async_computation.5 | async-start | bytes 1048576 | tf_op jit(solution)/shard_map/all_to_all | solution.py:143
  199.3 16.8 %all-to-all-start.3 = ((bf16[16,32,512]{2,1,0:T(8,128)(2,1)}), bf16[16,32,512]{2,1,0:T(8,128)(2,1)S(1)}, u32[]{:S(2)}, u32[]{:S(2)}) async-start(bf16[16,32,512]{2,1,0:T(8,128)(2,1)} %bitcast.81), calls=%async_computation.4 | async-start | bytes 1048576 | tf_op jit(solution)/shard_map/all_to_all | solution.py:150
Sparse Core Ops, SparseCore 0:
  10.2 59.6 all-gather.2
  106.3 28.4 all-gather.4
  161.1 38.2 reduce-scatter.1
where the time goes:
time: 226 us; the launch traced here: 225 us
  waiting for transfers between devices  75.2 us (33%)
  local copies, waits for them, and re-layouts  32.2 us (14%)
  blocking collectives  30.4 us (13%)
  matrix products  29.7 us (13%)
  starting transfers between devices  27.9 us (12%)
  other arithmetic  15.3 us (7%)
  between operations  14.3 us (6%)
    all_gather x1, waiting for transfers between devices, body(): rows_full = lax.all_gather(arrived, 'exp', axis=1, tiled=True)  28.4 us
    all_to_all x1, waiting for transfers between devices, body(): lax.all_to_all(pick_rows(attention_out, send_index, send_live), 'req', sp...  16.4 us
    dot_general x1, matrix products, body(): jnp.dot(active, w_down[0], preferred_element_type=jnp.float32)  16.2 us
    all_to_all x1, blocking collectives, body(): lax.all_to_all(outgoing, 'req', split_axis=0, concat_axis=0, tiled=True)  15.3 us
    psum x1, blocking collectives, body(): lax.psum(jnp.concatenate([squares[:, None], raw_logits], axis=1), 'exp')  15.1 us
    all_to_all x1, waiting for transfers between devices, body(): lax.all_to_all(pick_rows(page_rows, send_index, send_live), 'req', split_...  11.9 us
    dot_general x1, matrix products, body(): gate_h = jnp.dot(rows_full, w_gate[0], preferred_element_type=jnp.float32)  9.79 us
    scatter x1, local copies, waits for them, and re-layouts, body(): jnp.zeros((rows_all,), jnp.int32).at[came_from]  8.04 us
  transfers between devices with their start and end apart: 7, of which 7 were waited for; matrix products, arithmetic and copies ran while one was open for 18% of the time, Pallas kernels for 0%

commit v1 on v0

--- a/solution.py
+++ b/solution.py
@@ -120,7 +120,10 @@
     slot_live = jnp.any(chosen_slot, axis=2).reshape(-1)
     outgoing = pick_rows(normed_rows, slot_source, slot_live)
     arrived = lax.all_to_all(outgoing, "req", split_axis=0, concat_axis=0, tiled=True)
-    rows_full = lax.all_gather(arrived, "exp", axis=1, tiled=True)
+    peers = lax.axis_size("exp")
+    blocks = jnp.stack([arrived for _ in range(peers)])
+    blocks = lax.all_to_all(blocks, "exp", split_axis=0, concat_axis=0)
+    rows_full = jnp.concatenate(blocks, axis=1)
     gate_h = jnp.dot(rows_full, w_gate[0], preferred_element_type=jnp.float32)
     up_h = jnp.dot(rows_full, w_up[0], preferred_element_type=jnp.float32)
     active = (jax.nn.silu(gate_h) * up_h).astype(jnp.bfloat16)

time: 226 us -> 246 us (1.088)
  blocking collectives: 30.4 us -> 83.5 us
  waiting for transfers between devices: 75.2 us -> 44.9 us
  starting transfers between devices: 27.9 us -> 24.4 us
  local copies, waits for them, and re-layouts: 32.2 us -> 35.4 us
  matrix products: 29.7 us -> 27.2 us
    all_to_all x0 -> x1, blocking collectives: none -> 53.2 us  [body(): blocks = lax.all_to_all(blocks, 'exp', split_axis=0, concat_axis=0)]
    all_gather x1 -> x0, waiting for transfers between devices: 28.4 us -> none  [body(): rows_full = lax.all_gather(arrived, 'exp', axis=1, tiled=True)]
    all_to_all x1, starting transfers between devices: 6.81 us -> 3.57 us  [body(): lax.all_to_all(pick_rows(page_rows, send_index, send_live), 'req', split_...]
    dot_general x1, matrix products: 9.79 us -> 7.2 us  [body(): gate_h = jnp.dot(rows_full, w_gate[0], preferred_element_type=jnp.float32)]
    unnamed x23 -> x27, local copies, waits for them, and re-layouts: 4.74 us -> 6.72 us
  transfers between devices with their start and end apart: 7 -> 6, of which waited for: 7 -> 6; matrix products, arithmetic and copies ran while one was open for 18% -> 17% of each run, Pallas kernels for 0% -> 0%
where the time goes in v1:
time: 246 us; the launch traced here: 245 us
  blocking collectives  83.5 us (34%)
  waiting for transfers between devices  44.9 us (18%)
  local copies, waits for them, and re-layouts  35.4 us (14%)
  matrix products  27.2 us (11%)
  starting transfers between devices  24.4 us (10%)
  other arithmetic  15.3 us (6%)
  between operations  14.6 us (6%)
    all_to_all x1, blocking collectives, body(): blocks = lax.all_to_all(blocks, 'exp', split_axis=0, concat_axis=0)  53.2 us
    dot_general x1, matrix products, body(): jnp.dot(active, w_down[0], preferred_element_type=jnp.float32)  16.4 us
    all_to_all x1, waiting for transfers between devices, body(): lax.all_to_all(pick_rows(attention_out, send_index, send_live), 'req', sp...  15.7 us
    all_to_all x1, blocking collectives, body(): lax.all_to_all(outgoing, 'req', split_axis=0, concat_axis=0, tiled=True)  15.2 us
    psum x1, blocking collectives, body(): lax.psum(jnp.concatenate([squares[:, None], raw_logits], axis=1), 'exp')  15.1 us
    all_to_all x1, waiting for transfers between devices, body(): lax.all_to_all(pick_rows(page_rows, send_index, send_live), 'req', split_...  11.4 us
    scatter x1, local copies, waits for them, and re-layouts, body(): jnp.zeros((rows_all,), jnp.int32).at[came_from]  8.04 us
    all_to_all x1, waiting for transfers between devices, body(): lax.all_to_all(summed_value, 'req', split_axis=0, concat_axis=0, tiled=True)  7.51 us
  transfers between devices with their start and end apart: 6, of which 6 were waited for; matrix products, arithmetic and copies ran while one was open for 17% of the time, Pallas kernels for 0%

profile of v1, /device:TPU:0, one launch (start us, length us, event | category | flops | bytes accessed | tf_op | source)
XLA Modules:
  0.0 245.3 jit_solution(16116742093835065628)
XLA Ops:
  8.6 8.0 %scatter_custom_fusion = s32[2048]{0:T(1024)S(1)} fusion(s32[2048]{0:T(1024)S(1)} %compare_select_fusion.1, s32[2048]{0:T(1024)S(1)} %iota.72, s32[]{:T(128)} %constant.182.clone.1), kind=kCustom, calls=%fused_computation.94 | custom fusion | bytes 8196 | tf_op jit(solution)/shard_map/scatter | solution.py:43
  16.8 2.8 %select_reduce_fusion = s32[16,128]{0,1:T(8,128)S(1)} fusion(s32[16,128]{0,1:T(8,128)S(1)} %copy.119), kind=kOutput, calls=%fused_computation.27 | output fusion | flops 4388864 | bytes 16384 | tf_op jit(solution)/shard_map/jit(cumsum)/reduce_window_sum | solution.py:49
  20.6 1.6 gather_fusion.1
  23.1 7.1 %all-to-all-start = ((bf16[16,4,512]{2,1,0:T(4,128)(2,1)}), bf16[16,4,512]{2,1,0:T(4,128)(2,1)S(1)}, u32[]{:S(2)}, u32[]{:S(2)}) async-start(bf16[16,4,512]{2,1,0:T(4,128)(2,1)} %select_select_fusion.4), calls=%async_computation | async-start | bytes 131072 | tf_op jit(solution)/shard_map/all_to_all | solution.py:69
  38.0 7.0 %all-to-all-start.1 = ((bf16[16,4,4096]{2,1,0:T(4,128)(2,1)}), bf16[16,4,4096]{2,1,0:T(4,128)(2,1)S(1)}, u32[]{:S(2)}, u32[]{:S(2)}) async-start(bf16[16,4,4096]{2,1,0:T(4,128)(2,1)} %all_to_all.39), calls=%async_computation.1 | async-start | bytes 1048576 | tf_op jit(solution)/shard_map/all_to_all | solution.py:62
  45.5 1.5 gather_fusion.2
  47.0 15.7 %all-to-all-done.1 = bf16[16,4,4096]{2,1,0:T(4,128)(2,1)S(1)} async-done(((bf16[16,4,4096]{2,1,0:T(4,128)(2,1)}), bf16[16,4,4096]{2,1,0:T(4,128)(2,1)S(1)}, u32[]{:S(2)}, u32[]{:S(2)}) %all-to-all-start.1) | async-done | bytes 524320 | tf_op jit(solution)/shard_map/all_to_all | solution.py:62
  64.3 2.2 gather_fusion.7
  66.4 3.4 %all-gather.2.cloned.1.call-done = bf16[4096,512]{1,0:T(8,128)(2,1)} async-done(((bf16[256,512]{1,0:T(8,128)(2,1)}), bf16[4096,512]{1,0:T(8,128)(2,1)}) %all-gather.2.cloned.1.call-update) | async-done | bytes 4194320 | tf_op jit(solution)/shard_map/all_gather | solution.py:89
  69.8 3.4 %multiply_reduce_fusion = (f32[128]{0:T(128)S(1)}, f32[128,512]{1,0:T(8,128)S(1)}) fusion(bf16[4096,512]{1,0:T(8,128)(2,1)} %all-gather.2.cloned.1.call-done, bf16[128,4096]{1,0:T(8,128)(2,1)} %gather_fusion.7, pred[128]{0:T(512)(128)(4,1)S(1)} %get-tuple-element.8, bf16[128,512]{1,0:T(8,128)(2,1)S(1)} %copy-done.5), kind=kOutput, calls=%fused_computation.49 | convolution fusion | flops 537722752 | bytes 5636736 | tf_op jit(solution)/shard_map/dot_general | solution.py:87
  73.5 15.1 %psum.7 = f32[128,9]{0,1:T(8,128)S(1)} all-reduce(f32[128,9]{0,1:T(8,128)S(1)} %pad_maximum_fusion.3), channel_id=1, replica_groups=mesh['req'=16,'exp'=8] {'exp'}, use_global_device_ids=true, to_apply=%region_6.9 | all-reduce | flops 1152 | bytes 9216 | tf_op jit(solution)/shard_map/psum | solution.py:96
  88.7 2.0 gather_fusion.3
  90.9 15.2 %all_to_all.56 = bf16[16,32,512]{2,1,0:T(8,128)(2,1)S(1)} all-to-all(bf16[16,32,512]{2,1,0:T(8,128)(2,1)S(1)} %select_select_fusion.3), channel_id=1, replica_groups=mesh['req'=16,'exp'=8] {'req'}, dimensions={0} | all-to-all | bytes 1048576 | tf_op jit(solution)/shard_map/all_to_all | solution.py:122
  106.7 53.2 %all_to_all.57 = bf16[8,512,512]{1,2,0:T(8,128)(2,1)S(1)} all-to-all(bf16[8,512,512]{1,2,0:T(8,128)(2,1)S(1)} %stack.5), channel_id=1, replica_groups=mesh['req'=16,'exp'=8] {'exp'}, dimensions={0} | all-to-all | bytes 8388608 | tf_op jit(solution)/shard_map/all_to_all | solution.py:125
  159.9 2.0 copy-done.3
  161.8 7.2 %fusion.4 = f32[512,896]{1,0:T(8,128)S(1)} fusion(bf16[512,4096]{0,1:T(8,128)(2,1)S(1)} %bitcast.77, bf16[1,4096,896]{2,1,0:T(8,128)(2,1)} %param.27), kind=kOutput, calls=%fused_computation.15 | convolution fusion | flops 3758096384 | bytes 13369344 | tf_op jit(solution)/shard_map/dot_general | solution.py:127
  169.0 16.4 %fusion.6 = bf16[512,4096]{1,0:T(8,128)(2,1)} fusion(bf16[1,896,4096]{2,1,0:T(8,128)(2,1)} %param.29, f32[512,896]{1,0:T(8,128)S(1)} %fusion.4, bf16[512,4096]{0,1:T(8,128)(2,1)} %bitcast.78, bf16[1,4096,896]{2,1,0:T(8,128)(2,1)} %param.28), kind=kOutput, calls=%fused_computation.17 | convolution fusion | flops 7521042432 | bytes 24903680 | tf_op jit(solution)/shard_map/dot_general | solution.py:131
  191.4 1.4 select_select_fusion
  194.9 3.6 %all-to-all-start.5 = ((bf16[16,4,4096]{2,1,0:T(4,128)(2,1)}), bf16[16,4,4096]{2,1,0:T(4,128)(2,1)S(1)}, u32[]{:S(2)}, u32[]{:S(2)}) async-start(bf16[16,4,4096]{2,1,0:T(4,128)(2,1)} %all_to_all.47), calls=%async_computation.6 | async-start | bytes 1048576 | tf_op jit(solution)/shard_map/all_to_all | solution.py:146
  198.5 11.4 %all-to-all-done.5 = bf16[16,4,4096]{2,1,0:T(4,128)(2,1)S(1)} async-done(((bf16[16,4,4096]{2,1,0:T(4,128)(2,1)}), bf16[16,4,4096]{2,1,0:T(4,128)(2,1)S(1)}, u32[]{:S(2)}, u32[]{:S(2)}) %all-to-all-start.5) | async-done | bytes 524320 | tf_op jit(solution)/shard_map/all_to_all | solution.py:146
  211.3 2.2 gather_fusion.9
  213.5 5.9 %reduce-scatter.2.cloned.1.call-done = bf16[512,512]{1,0:T(8,128)(2,1)} async-done(((bf16[512,4096]{1,0:T(8,128)(2,1)}), bf16[512,512]{1,0:T(8,128)(2,1)}) %reduce-scatter.2.cloned.1.call-update) | async-done | bytes 524304 | tf_op jit(solution)/shard_map/reduce_scatter | solution.py:134
  219.4 6.7 %all-to-all-start.4 = ((bf16[16,32,512]{2,1,0:T(8,128)(2,1)}), bf16[16,32,512]{2,1,0:T(8,128)(2,1)S(1)}, u32[]{:S(2)}, u32[]{:S(2)}) async-start(bf16[16,32,512]{2,1,0:T(8,128)(2,1)} %bitcast.86), calls=%async_computation.5 | async-start | bytes 1048576 | tf_op jit(solution)/shard_map/all_to_all | solution.py:153
  228.7 7.5 %all-to-all-done.4 = bf16[16,32,512]{2,1,0:T(8,128)(2,1)S(1)} async-done(((bf16[16,32,512]{2,1,0:T(8,128)(2,1)}), bf16[16,32,512]{2,1,0:T(8,128)(2,1)S(1)}, u32[]{:S(2)}, u32[]{:S(2)}) %all-to-all-start.4) | async-done | bytes 524320 | tf_op jit(solution)/shard_map/all_to_all | solution.py:153
  (125 shorter events, 28.4 us)
Async XLA Ops:
  7.2 182.9 %copy-start = (bf16[256,8,256]{2,1,0:T(8,128)(2,1)S(1)}, bf16[256,8,256]{2,1,0:T(8,128)(2,1)}, u32[]{:S(2)}) copy-start(bf16[256,8,256]{2,1,0:T(8,128)(2,1)} %param.22) | copy-start | bytes 3145732
  7.2 24.4 %copy-start.2 = (bf16[128,4096]{1,0:T(8,128)(2,1)S(1)}, bf16[128,4096]{1,0:T(8,128)(2,1)}, u32[]{:S(2)}) copy-start(bf16[128,4096]{1,0:T(8,128)(2,1)} %param.17) | copy-start | bytes 3145732
  7.2 62.6 %all-gather.2.cloned.1.call-start = ((), (), s32[]{:S(2)}) async-start(), calls=%async_computation.7 | async-start | bytes 4456448 | tf_op jit(solution)/shard_map/all_gather | solution.py:89
  23.1 14.9 %all-to-all-start = ((bf16[16,4,512]{2,1,0:T(4,128)(2,1)}), bf16[16,4,512]{2,1,0:T(4,128)(2,1)S(1)}, u32[]{:S(2)}, u32[]{:S(2)}) async-start(bf16[16,4,512]{2,1,0:T(4,128)(2,1)} %select_select_fusion.4), calls=%async_computation | async-start | bytes 131072 | tf_op jit(solution)/shard_map/all_to_all | solution.py:69
  31.5 13.9 %copy-start.4 = (bf16[128,512]{1,0:T(8,128)(2,1)S(1)}, bf16[128,512]{1,0:T(8,128)(2,1)}, u32[]{:S(2)}) copy-start(bf16[128,512]{1,0:T(8,128)(2,1)} %param.18) | copy-start | bytes 393220
  38.0 24.7 %all-to-all-start.1 = ((bf16[16,4,4096]{2,1,0:T(4,128)(2,1)}), bf16[16,4,4096]{2,1,0:T(4,128)(2,1)S(1)}, u32[]{:S(2)}, u32[]{:S(2)}) async-start(bf16[16,4,4096]{2,1,0:T(4,128)(2,1)} %all_to_all.39), calls=%async_computation.1 | async-start | bytes 1048576 | tf_op jit(solution)/shard_map/all_to_all | solution.py:62
  45.0 174.4 %reduce-scatter.2.cloned.1.call-start = ((), (), s32[]{:S(2)}) async-start(), calls=%async_computation.8 | async-start | bytes 4718592 | tf_op jit(solution)/shard_map/reduce_scatter | solution.py:134
  64.2 5.6 %copy-start.5 = (bf16[128,512]{1,0:T(8,128)(2,1)S(1)}, bf16[128,512]{1,0:T(8,128)(2,1)}, u32[]{:S(2)}) copy-start(bf16[128,512]{1,0:T(8,128)(2,1)} %gather_fusion.2) | copy-start | bytes 393220
  66.4 6.8 %copy-start.6 = (f32[512,8]{0,1:T(8,128)S(1)}, f32[512,8]{0,1:T(8,128)}, u32[]{:S(2)}) copy-start(f32[512,8]{0,1:T(8,128)} %param.20) | copy-start | bytes 49156
  66.4 6.8 %copy-start.8 = (f32[512]{0:T(512)S(1)}, f32[512]{0:T(512)}, u32[]{:S(2)}) copy-start(f32[512]{0:T(512)} %param.21) | copy-start | bytes 6148
  159.9 2.0 copy-start.3
  185.4 0.7 copy-start.9
  185.4 1.0 copy-start.10
  185.4 4.6 %copy-start.7 = (s32[128,2]{0,1:T(2,128)S(1)}, s32[128,2]{0,1:T(2,128)}, u32[]{:S(2)}) copy-start(s32[128,2]{0,1:T(2,128)} %param.26) | copy-start | bytes 3076
  192.8 17.0 %copy-start.1 = (bf16[128,4096]{1,0:T(8,128)(2,1)}, bf16[128,4096]{1,0:T(8,128)(2,1)S(1)}, u32[]{:S(2)}) copy-start(bf16[128,4096]{1,0:T(8,128)(2,1)S(1)} %select_select_fusion) | copy-start | bytes 3145732
  194.9 15.0 %all-to-all-start.5 = ((bf16[16,4,4096]{2,1,0:T(4,128)(2,1)}), bf16[16,4,4096]{2,1,0:T(4,128)(2,1)S(1)}, u32[]{:S(2)}, u32[]{:S(2)}) async-start(bf16[16,4,4096]{2,1,0:T(4,128)(2,1)} %all_to_all.47), calls=%async_computation.6 | async-start | bytes 1048576 | tf_op jit(solution)/shard_map/all_to_all | solution.py:146
  219.4 16.8 %all-to-all-start.4 = ((bf16[16,32,512]{2,1,0:T(8,128)(2,1)}), bf16[16,32,512]{2,1,0:T(8,128)(2,1)S(1)}, u32[]{:S(2)}, u32[]{:S(2)}) async-start(bf16[16,32,512]{2,1,0:T(8,128)(2,1)} %bitcast.86), calls=%async_computation.5 | async-start | bytes 1048576 | tf_op jit(solution)/shard_map/all_to_all | solution.py:153
Sparse Core Ops, SparseCore 0:
  10.2 59.6 all-gather.1
  185.6 33.7 reduce-scatter.1
